TPU v7x, 32 devices: a whole 2x2x4 slice. The times are simulated.
32 devices in a mesh: coord: 8 (over z, y), cohort: 4 (over x, core).
Axes of the slice: x: 2, y: 2, z: 4, core: 2. Of those that a mesh axis runs over, the one named last changes fastest.
Arguments:
- shapes: bfloat16 [4, 1024, 32768], P('cohort', None, 'coord'), may hold values from -6 to 6
- sketch_signs: int32 [4, 1024, 128], P('cohort'), may hold values from -1 to 1
- merge_sketch: float32 [2, 2, 128, 128], replicated, may hold values from -1.5 to 1.5
Outputs:
- basis: float32 [4, 32768, 128], P('cohort', 'coord')
- scores: float32 [4, 1024, 128], P('cohort', 'coord')
All inputs are finite; a program needn't handle non-finite values.
Results may differ from a plain program's by a relative error of at most 0.0086.
Values sent between devices are 32-bit elements; how exact they have to be, the bound alone decides.
A program may use at most 64 MiB of HBM per device.

v0:
```python
import math
import jax
import jax.numpy as jnp
from jax import lax
from jax.sharding import PartitionSpec as P

LEVELS = 2


def from_partner(shard, axis, distance):
    return lax.ppermute(shard, axis, [(i, i ^ 1 << distance) for i in range(lax.axis_size(axis))])


def lower_inverse(gram):
    factor = jnp.linalg.cholesky(gram)
    ident = jnp.eye(gram.shape[0], dtype=gram.dtype)
    inverse = jax.scipy.linalg.solve_triangular(factor, ident, lower=True)
    return inverse.T


def inverse_all(gram):
    return lower_inverse(gram)


def orthonormal(mixed):
    gram = jnp.einsum("...pk,...pl->...kl", mixed, mixed, precision=lax.Precision.HIGHEST)
    gram = lax.psum(gram, "coord")
    return jnp.matmul(mixed, inverse_all(gram), precision=lax.Precision.HIGHEST)


def on_device(shapes, sketch_signs, merge_sketch):
    data = shapes[0].astype(jnp.float32)
    centered = (data - jnp.mean(data, axis=0, keepdims=True)).astype(jnp.bfloat16)
    signs = sketch_signs[0].astype(jnp.bfloat16)
    sketch = lax.dot_general(
        centered, signs, (((0,), (0,)), ((), ())), preferred_element_type=jnp.float32
    )
    current = orthonormal(sketch)
    position = lax.axis_index("cohort")
    for level in range(LEVELS):
        partner = from_partner(current, "cohort", level)
        upper_side = position >> level & 1 == 1
        lower_basis = jnp.where(upper_side, partner, current)
        upper_basis = jnp.where(upper_side, current, partner)
        mixed = jnp.matmul(lower_basis, merge_sketch[level, 0], precision=lax.Precision.HIGHEST)
        mixed = mixed + jnp.matmul(
            upper_basis, merge_sketch[level, 1], precision=lax.Precision.HIGHEST
        )
        current = orthonormal(mixed)
    width = current.shape[1]
    total_coords = current.shape[0] * lax.axis_size("coord")
    rounded = current.astype(jnp.bfloat16)
    sums = lax.psum_scatter(
        jnp.dot(centered, rounded, preferred_element_type=jnp.float32),
        "coord",
        scatter_dimension=0,
        tiled=True,
    )
    factor = 4.0 * math.sqrt(width / total_coords)
    basis_out = current * math.sqrt(total_coords)
    return (basis_out[None], (sums * factor)[None])


def solution(mesh):
    placed = (P("cohort", None, "coord"), P("cohort", None, None), P())
    return jax.shard_map(
        on_device,
        mesh=mesh,
        in_specs=placed,
        out_specs=(P("cohort", "coord", None), P("cohort", "coord", None)),
        check_vma=False,
    )
```

profile of v0, /device:TPU:0, one launch (start us, length us, event | category | flops | bytes accessed | tf_op | source)
XLA Modules:
  0.0 468.8 jit_solution(535079962595938200)
XLA Ops:
  7.2 4.7 %convert_reduce_fusion = f32[4096]{0:T(1024)S(1)} fusion(bf16[1,1024,4096]{2,1,0:T(8,128)(2,1)} %param.6), kind=kLoop, calls=%fused_computation.2 | loop fusion | flops 8384512 | bytes 8404992 | tf_op jit(solution)/shard_map/reduce_sum | solution.py:33
  12.0 1.0 copy-done
  13.0 3.8 fusion.6
  16.8 4.1 fusion.46
  21.4 71.6 %all-reduce.4.cloned.1.call-done = f32[128,128]{0,1:T(8,128)} async-done(((f32[128,128]{0,1:T(8,128)}), f32[128,128]{0,1:T(8,128)}) %all-reduce.4.cloned.1.call-update) | async-done | bytes 65552 | tf_op jit(solution)/shard_map/psum | solution.py:27
  94.8 11.7 %cholesky.59 = f32[128,128]{1,0:T(8,128)S(1)} custom-call(f32[128,128]{1,0:T(8,128)S(1)} %fusion.41), custom_call_target="Cholesky" | custom-call | tf_op jit(solution)/shard_map/jit(cholesky)/cholesky | solution.py:15
  107.9 9.8 %custom-call.7 = f32[1,128,128]{1,2,0:T(8,128)S(1)} custom-call(f32[1,128,128]{2,1,0:T(8,128)S(1)} %fusion.29), custom_call_target="InvertDiagBlocksLowerTriangular" | custom-call | tf_op jit(solution)/shard_map/jit(_solve_triangular)/triangular_solve | solution.py:17
  118.0 3.1 fusion.47
  121.1 4.4 collective-permute-done
  125.5 1.3 copy-done.1
  126.8 1.9 fusion.13
  128.7 3.4 convolution_add_fusion.1
  132.2 4.1 fusion.48
  136.3 70.6 %all-reduce.6.cloned.1.call-done = f32[128,128]{0,1:T(8,128)} async-done(((f32[128,128]{0,1:T(8,128)}), f32[128,128]{0,1:T(8,128)}) %all-reduce.6.cloned.1.call-update) | async-done | bytes 65552 | tf_op jit(solution)/shard_map/psum | solution.py:27
  208.8 11.7 %cholesky.70 = f32[128,128]{1,0:T(8,128)S(1)} custom-call(f32[128,128]{1,0:T(8,128)S(1)} %fusion.37), custom_call_target="Cholesky" | custom-call | tf_op jit(solution)/shard_map/jit(cholesky)/cholesky | solution.py:15
  221.8 9.8 %custom-call.8 = f32[1,128,128]{1,2,0:T(8,128)S(1)} custom-call(f32[1,128,128]{2,1,0:T(8,128)S(1)} %fusion.30), custom_call_target="InvertDiagBlocksLowerTriangular" | custom-call | tf_op jit(solution)/shard_map/jit(_solve_triangular)/triangular_solve | solution.py:17
  231.9 3.1 fusion.49
  235.0 1.5 collective-permute-start.1
  236.5 44.3 %collective-permute-done.1 = f32[4096,128]{1,0:T(8,128)S(1)} collective-permute-done((f32[4096,128]{1,0:T(8,128)}, f32[4096,128]{1,0:T(8,128)S(1)}, u32[]{:S(2)}, u32[]{:S(2)}) %collective-permute-start.1) | collective-permute-done | bytes 2097184 | tf_op jit(solution)/shard_map/ppermute | solution.py:11
  280.8 1.3 copy-done.2
  282.1 1.9 fusion.10
  284.0 3.5 convolution_add_fusion
  287.5 4.1 fusion.50
  291.6 70.8 %all-reduce.8.cloned.1.call-done = f32[128,128]{0,1:T(8,128)} async-done(((f32[128,128]{0,1:T(8,128)}), f32[128,128]{0,1:T(8,128)}) %all-reduce.8.cloned.1.call-update) | async-done | bytes 65552 | tf_op jit(solution)/shard_map/psum | solution.py:27
  364.3 11.7 %cholesky.81 = f32[128,128]{1,0:T(8,128)S(1)} custom-call(f32[128,128]{1,0:T(8,128)S(1)} %fusion.33), custom_call_target="Cholesky" | custom-call | tf_op jit(solution)/shard_map/jit(cholesky)/cholesky | solution.py:15
  377.3 9.8 %custom-call.9 = f32[1,128,128]{1,2,0:T(8,128)S(1)} custom-call(f32[1,128,128]{2,1,0:T(8,128)S(1)} %fusion.31), custom_call_target="InvertDiagBlocksLowerTriangular" | custom-call | tf_op jit(solution)/shard_map/jit(_solve_triangular)/triangular_solve | solution.py:17
  387.4 1.9 fusion.51
  389.4 1.3 copy-done.3
  390.7 6.5 %fusion.3 = f32[1024,128]{1,0:T(8,128)} fusion(bf16[1,1024,4096]{2,1,0:T(8,128)(2,1)} %param.6, f32[4096]{0:T(1024)S(1)} %broadcast_multiply_fusion, f32[4096,128]{1,0:T(8,128)S(1)} %fusion.51), kind=kOutput, calls=%fused_computation.6 | convolution fusion | flops 1086849024 | bytes 11026432 | tf_op jit(solution)/shard_map/dot_general | solution.py:54
  397.2 3.1 multiply_bitcast_fusion
  400.3 60.1 %reduce-scatter.2.cloned.1.call-done = f32[128,128]{1,0:T(8,128)} async-done(((f32[1024,128]{1,0:T(8,128)}), f32[128,128]{1,0:T(8,128)}) %reduce-scatter.2.cloned.1.call-update) | async-done | bytes 65552 | tf_op jit(solution)/shard_map/reduce_scatter | solution.py:53
  460.4 1.5 multiply_bitcast_fusion.1
  (34 shorter events, 10.9 us)
Async XLA Ops:
  7.2 85.9 %all-reduce.4.cloned.1.call-start = ((), (), s32[]{:S(2)}) async-start(), calls=%async_computation.1 | async-start | bytes 131072 | tf_op jit(solution)/shard_map/psum | solution.py:27
  7.2 5.8 %copy-start = (bf16[1,1024,4096]{2,1,0:T(8,128)(2,1)S(1)}, bf16[1,1024,4096]{2,1,0:T(8,128)(2,1)}, u32[]{:S(2)}) copy-start(bf16[1,1024,4096]{2,1,0:T(8,128)(2,1)} %param.6) | copy-start | bytes 25165828
  20.9 186.1 %all-reduce.6.cloned.1.call-start = ((), (), s32[]{:S(2)}) async-start(), calls=%async_computation.2 | async-start | bytes 131072 | tf_op jit(solution)/shard_map/psum | solution.py:27
  118.0 8.9 %copy-start.4 = (f32[2,2,128,128]{3,2,1,0:T(8,128)S(1)}, f32[2,2,128,128]{3,2,1,0:T(8,128)}, u32[]{:S(2)}) copy-start(f32[2,2,128,128]{3,2,1,0:T(8,128)} %param.8) | copy-start | bytes 786436
  121.1 4.4 collective-permute-start
  125.5 1.4 copy-start.1
  136.3 226.2 %all-reduce.8.cloned.1.call-start = ((), (), s32[]{:S(2)}) async-start(), calls=%async_computation.3 | async-start | bytes 131072 | tf_op jit(solution)/shard_map/psum | solution.py:27
  235.0 45.7 %collective-permute-start.1 = (f32[4096,128]{1,0:T(8,128)}, f32[4096,128]{1,0:T(8,128)S(1)}, u32[]{:S(2)}, u32[]{:S(2)}) collective-permute-start(f32[4096,128]{1,0:T(8,128)} %fusion.49), channel_id=1, source_target_pairs={{0,2},{1,3},{2,0},{3,1},{4,6},{5,7},{6,4},{7,5},{8,10},{9,11},{10,... | collective-permute-start | bytes 6291464 | tf_op jit(solution)/shard_map/ppermute | solution.py:11
  280.8 1.4 copy-start.2
  291.6 168.8 %reduce-scatter.2.cloned.1.call-start = ((), (), s32[]{:S(2)}) async-start(), calls=%async_computation.4 | async-start | bytes 589824 | tf_op jit(solution)/shard_map/reduce_scatter | solution.py:53
  389.3 1.3 copy-start.3
Sparse Core Ops, SparseCore 0:
  21.0 71.9 all-reduce.3
  136.4 70.5 all-reduce.5
  291.7 70.7 all-reduce.7
  397.3 63.0 reduce-scatter.1
where the time goes:
time: 475 us; the launch traced here: 469 us
  waiting for transfers between devices  322 us (68%)
  other arithmetic  80.4 us (17%)
  matrix products  42.3 us (9%)
  between operations  14.3 us (3%)
  local copies, waits for them, and re-layouts  7.82 us (2%)
    psum x3, waiting for transfers between devices, orthonormal(): gram = lax.psum(gram, 'coord')  213 us
    reduce_scatter x1, waiting for transfers between devices, on_device(): lax.psum_scatter(jnp.dot(centered, rounded, preferred_element_type=jnp.fl...  60.1 us
    ppermute x2, waiting for transfers between devices, from_partner(): lax.ppermute(shard, axis, [(i, i ^ 1 << distance) for i in range(lax.axis...  48.6 us
    another operation x9, other arithmetic, lower_inverse(): factor = jnp.linalg.cholesky(gram)  37.2 us
    another operation x6, other arithmetic, lower_inverse(): inverse = jax.scipy.linalg.solve_triangular(factor, ident, lower=True)  31.4 us
    dot_general x3, matrix products, orthonormal(): jnp.einsum('...pk,...pl->...kl', mixed, mixed, precision=lax.Precision.HI...  12.3 us
  transfers between devices with their start and end apart: 6, of which 6 were waited for; matrix products, arithmetic and copies ran while one was open for 1% of the time, Pallas kernels for 0%

commit v1 on v0

--- a/solution.py
+++ b/solution.py
@@ -24,7 +24,7 @@
 
 def orthonormal(mixed):
     gram = jnp.einsum("...pk,...pl->...kl", mixed, mixed, precision=lax.Precision.HIGHEST)
-    gram = lax.psum(gram, "coord")
+    gram = jnp.sum(lax.all_gather(gram, "coord"), axis=0)
     return jnp.matmul(mixed, inverse_all(gram), precision=lax.Precision.HIGHEST)
 
 

time: 475 us -> 349 us (0.73)
  waiting for transfers between devices: 322 us -> 106 us
  blocking collectives: 0 us -> 96.1 us
    psum x3 -> x0, waiting for transfers between devices: 213 us -> none  [orthonormal(): gram = lax.psum(gram, 'coord')]
    all_gather x0 -> x3, blocking collectives: none -> 96.1 us  [orthonormal(): gram = jnp.sum(lax.all_gather(gram, 'coord'), axis=0)]
    ppermute x2, waiting for transfers between devices: 48.6 us -> 43.2 us  [from_partner(): lax.ppermute(shard, axis, [(i, i ^ 1 << distance) for i in range(lax.axis...]
  transfers between devices with their start and end apart: 6 -> 3, of which waited for: 6 -> 3; matrix products, arithmetic and copies ran while one was open for 1% -> 1% of each run, Pallas kernels for 0% -> 0%
where the time goes in v1:
time: 349 us; the launch traced here: 343 us
  waiting for transfers between devices  106 us (30%)
  blocking collectives  96.1 us (28%)
  other arithmetic  78 us (22%)
  matrix products  42.4 us (12%)
  between operations  14.7 us (4%)
  local copies, waits for them, and re-layouts  3.97 us (1%)
    all_gather x3, blocking collectives, orthonormal(): gram = jnp.sum(lax.all_gather(gram, 'coord'), axis=0)  96.1 us
    reduce_scatter x1, waiting for transfers between devices, on_device(): lax.psum_scatter(jnp.dot(centered, rounded, preferred_element_type=jnp.fl...  63 us
    ppermute x2, waiting for transfers between devices, from_partner(): lax.ppermute(shard, axis, [(i, i ^ 1 << distance) for i in range(lax.axis...  43.2 us
    another operation x9, other arithmetic, lower_inverse(): factor = jnp.linalg.cholesky(gram)  37.2 us
    another operation x6, other arithmetic, lower_inverse(): inverse = jax.scipy.linalg.solve_triangular(factor, ident, lower=True)  31.4 us
    dot_general x3, matrix products, orthonormal(): jnp.einsum('...pk,...pl->...kl', mixed, mixed, precision=lax.Precision.HI...  10.5 us
    dot_general x3, matrix products, orthonormal(): return jnp.matmul(mixed, inverse_all(gram), precision=lax.Precision.HIGHEST)  8.47 us
  transfers between devices with their start and end apart: 3, of which 3 were waited for; matrix products, arithmetic and copies ran while one was open for 1% of the time, Pallas kernels for 0%

profile of v1, /device:TPU:0, one launch (start us, length us, event | category | flops | bytes accessed | tf_op | source)
XLA Modules:
  0.0 343.0 jit_solution(11687555814793687419)
XLA Ops:
  7.2 4.7 %convert_reduce_fusion = f32[4096]{0:T(1024)S(1)} fusion(bf16[1,1024,4096]{2,1,0:T(8,128)(2,1)} %param.6), kind=kLoop, calls=%fused_computation.2 | loop fusion | flops 8384512 | bytes 8404992 | tf_op jit(solution)/shard_map/reduce_sum | solution.py:33
  12.0 1.0 copy-done.2
  13.0 3.8 %fusion.6 = f32[4096,128]{1,0:T(8,128)S(1)} fusion(bf16[1,1024,4096]{2,1,0:T(8,128)(2,1)S(1)} %copy-done.2, f32[4096]{0:T(1024)S(1)} %broadcast_multiply_fusion, s32[1,1024,128]{2,1,0:T(8,128)} %param.7), kind=kOutput, calls=%fused_computation.8 | convolution fusion | flops 1086455808 | bytes 11026432 | tf_op jit(solution)/shard_map/dot_general | solution.py:35
  16.8 3.6 %fusion.46 = f32[128,128]{1,0:T(8,128)S(1)} fusion(f32[4096,128]{1,0:T(8,128)S(1)} %fusion.6), kind=kOutput, calls=%fused_computation.66 | convolution fusion | flops 805306368 | bytes 2162688 | tf_op jit(solution)/shard_map/...pk,...pl->...kl/dot_general | solution.py:26
  20.4 33.5 %all-gather = f32[1024,128]{1,0:T(8,128)S(1)} all-gather(f32[128,128]{1,0:T(8,128)S(1)} %fusion.46), channel_id=2, replica_groups=mesh['coord'=8,'cohort'=4] {'coord'}, dimensions={0}, use_global_device_ids=true | all-gather | bytes 589824 | tf_op jit(solution)/shard_map/all_gather | solution.py:27
  54.1 11.7 %cholesky.59 = f32[128,128]{1,0:T(8,128)S(1)} custom-call(f32[128,128]{1,0:T(8,128)S(1)} %fusion.41), custom_call_target="Cholesky" | custom-call | tf_op jit(solution)/shard_map/jit(cholesky)/cholesky | solution.py:15
  67.1 9.8 %custom-call.7 = f32[1,128,128]{1,2,0:T(8,128)S(1)} custom-call(f32[1,128,128]{2,1,0:T(8,128)S(1)} %fusion.29), custom_call_target="InvertDiagBlocksLowerTriangular" | custom-call | tf_op jit(solution)/shard_map/jit(_solve_triangular)/triangular_solve | solution.py:17
  77.3 3.4 %fusion.47 = f32[4096,128]{1,0:T(8,128)S(1)} fusion(f32[4096,128]{1,0:T(8,128)} %copy-done.1, f32[128,128]{1,0:T(8,128)S(1)} %fusion.27), kind=kOutput, calls=%fused_computation.67 | convolution fusion | flops 805306368 | bytes 4259840 | tf_op jit(solution)/shard_map/dot_general | solution.py:28
  80.8 4.3 %collective-permute-done = f32[4096,128]{1,0:T(8,128)} collective-permute-done((f32[4096,128]{1,0:T(8,128)S(1)}, f32[4096,128]{1,0:T(8,128)}, u32[]{:S(2)}, u32[]{:S(2)}) %collective-permute-start) | collective-permute-done | bytes 2097184 | tf_op jit(solution)/shard_map/ppermute | solution.py:11
  85.1 3.5 %fusion.13 = f32[4096,128]{1,0:T(8,128)S(1)} fusion(f32[4096,128]{1,0:T(8,128)S(1)} %fusion.47, f32[4096,128]{1,0:T(8,128)} %collective-permute-done, pred[]{:T(512)S(6)} %eq.16, f32[2,2,128,128]{3,2,1,0:T(8,128)S(1)} %copy-done.5), kind=kOutput, calls=%fused_computation.17 | convolution fusion | flops 805830656 | bytes 6356993 | tf_op jit(solution)/shard_map/dot_general | solution.py:46
  88.5 3.4 %convolution_add_fusion.1 = f32[4096,128]{1,0:T(8,128)S(1)} fusion(f32[4096,128]{1,0:T(8,128)S(1)} %fusion.13, f32[4096,128]{1,0:T(8,128)} %collective-permute-done, f32[4096,128]{1,0:T(8,128)} %copy-done, pred[]{:T(512)S(6)} %eq.16, f32[2,2,128,128]{3,2,1,0:T(8,128)S(1)} %copy-done.5), kind=kOutput, calls=%fused_computation.12 | convolution fusion | flops 806354944 | bytes 8454145 | tf_op jit(solution)/shard_map/dot_general | solution.py:45
  92.0 3.5 %fusion.48 = f32[128,128]{1,0:T(8,128)S(1)} fusion(f32[4096,128]{1,0:T(8,128)S(1)} %convolution_add_fusion.1), kind=kOutput, calls=%fused_computation.68 | convolution fusion | flops 805306368 | bytes 2162688 | tf_op jit(solution)/shard_map/...pk,...pl->...kl/dot_general | solution.py:26
  95.4 31.4 %all-gather.1 = f32[1024,128]{1,0:T(8,128)S(1)} all-gather(f32[128,128]{1,0:T(8,128)S(1)} %fusion.48), channel_id=3, replica_groups=mesh['coord'=8,'cohort'=4] {'coord'}, dimensions={0}, use_global_device_ids=true | all-gather | bytes 589824 | tf_op jit(solution)/shard_map/all_gather | solution.py:27
  127.0 11.7 %cholesky.70 = f32[128,128]{1,0:T(8,128)S(1)} custom-call(f32[128,128]{1,0:T(8,128)S(1)} %fusion.37), custom_call_target="Cholesky" | custom-call | tf_op jit(solution)/shard_map/jit(cholesky)/cholesky | solution.py:15
  139.3 0.7 fusion.30
  140.0 9.8 %custom-call.8 = f32[1,128,128]{1,2,0:T(8,128)S(1)} custom-call(f32[1,128,128]{2,1,0:T(8,128)S(1)} %fusion.30), custom_call_target="InvertDiagBlocksLowerTriangular" | custom-call | tf_op jit(solution)/shard_map/jit(_solve_triangular)/triangular_solve | solution.py:17
  150.1 3.1 fusion.49
  153.2 1.5 collective-permute-start.1
  154.7 38.9 %collective-permute-done.1 = f32[4096,128]{1,0:T(8,128)S(1)} collective-permute-done((f32[4096,128]{1,0:T(8,128)}, f32[4096,128]{1,0:T(8,128)S(1)}, u32[]{:S(2)}, u32[]{:S(2)}) %collective-permute-start.1) | collective-permute-done | bytes 2097184 | tf_op jit(solution)/shard_map/ppermute | solution.py:11
  193.6 1.3 copy-done.3
  195.0 1.9 fusion.10
  196.9 3.5 %convolution_add_fusion = f32[4096,128]{1,0:T(8,128)S(1)} fusion(f32[4096,128]{1,0:T(8,128)S(1)} %fusion.10, f32[4096,128]{1,0:T(8,128)} %copy-done.3, f32[4096,128]{1,0:T(8,128)} %fusion.49, pred[]{:T(512)S(6)} %eq.15, f32[2,2,128,128]{3,2,1,0:T(8,128)S(1)} %copy-done.5), kind=kOutput, calls=%fused_computation.11 | convolution fusion | flops 806354944 | bytes 8454145 | tf_op jit(solution)/shard_map/dot_general | solution.py:45
  200.3 3.5 %fusion.50 = f32[128,128]{1,0:T(8,128)S(1)} fusion(f32[4096,128]{1,0:T(8,128)S(1)} %convolution_add_fusion), kind=kOutput, calls=%fused_computation.70 | convolution fusion | flops 805306368 | bytes 2162688 | tf_op jit(solution)/shard_map/...pk,...pl->...kl/dot_general | solution.py:26
  203.8 31.2 %all-gather.2 = f32[1024,128]{1,0:T(8,128)S(1)} all-gather(f32[128,128]{1,0:T(8,128)S(1)} %fusion.50), channel_id=4, replica_groups=mesh['coord'=8,'cohort'=4] {'coord'}, dimensions={0}, use_global_device_ids=true | all-gather | bytes 589824 | tf_op jit(solution)/shard_map/all_gather | solution.py:27
  235.2 11.7 %cholesky.81 = f32[128,128]{1,0:T(8,128)S(1)} custom-call(f32[128,128]{1,0:T(8,128)S(1)} %fusion.33), custom_call_target="Cholesky" | custom-call | tf_op jit(solution)/shard_map/jit(cholesky)/cholesky | solution.py:15
  248.2 9.8 %custom-call.9 = f32[1,128,128]{1,2,0:T(8,128)S(1)} custom-call(f32[1,128,128]{2,1,0:T(8,128)S(1)} %fusion.31), custom_call_target="InvertDiagBlocksLowerTriangular" | custom-call | tf_op jit(solution)/shard_map/jit(_solve_triangular)/triangular_solve | solution.py:17
  258.3 1.9 fusion.51
  260.3 1.3 copy-done.4
  261.6 6.5 %fusion.3 = f32[1024,128]{1,0:T(8,128)} fusion(bf16[1,1024,4096]{2,1,0:T(8,128)(2,1)} %param.6, f32[4096]{0:T(1024)S(1)} %broadcast_multiply_fusion, f32[4096,128]{1,0:T(8,128)S(1)} %fusion.51), kind=kOutput, calls=%fused_computation.6 | convolution fusion | flops 1086849024 | bytes 11026432 | tf_op jit(solution)/shard_map/dot_general | solution.py:54
  268.1 3.1 multiply_bitcast_fusion
  271.2 63.0 %reduce-scatter.2.cloned.1.call-done = f32[128,128]{1,0:T(8,128)} async-done(((f32[1024,128]{1,0:T(8,128)}), f32[128,128]{1,0:T(8,128)}) %reduce-scatter.2.cloned.1.call-update) | async-done | bytes 65552 | tf_op jit(solution)/shard_map/reduce_scatter | solution.py:53
  334.3 1.5 multiply_bitcast_fusion.1
  (33 shorter events, 4.8 us)
Async XLA Ops:
  7.2 327.1 %reduce-scatter.2.cloned.1.call-start = ((), (), s32[]{:S(2)}) async-start(), calls=%async_computation.1 | async-start | bytes 589824 | tf_op jit(solution)/shard_map/reduce_scatter | solution.py:53
  7.2 5.8 %copy-start.2 = (bf16[1,1024,4096]{2,1,0:T(8,128)(2,1)S(1)}, bf16[1,1024,4096]{2,1,0:T(8,128)(2,1)}, u32[]{:S(2)}) copy-start(bf16[1,1024,4096]{2,1,0:T(8,128)(2,1)} %param.6) | copy-start | bytes 25165828
  16.8 3.6 %copy-start.1 = (f32[4096,128]{1,0:T(8,128)}, f32[4096,128]{1,0:T(8,128)S(1)}, u32[]{:S(2)}) copy-start(f32[4096,128]{1,0:T(8,128)S(1)} %fusion.6) | copy-start | bytes 6291460
  77.2 7.8 %copy-start.5 = (f32[2,2,128,128]{3,2,1,0:T(8,128)S(1)}, f32[2,2,128,128]{3,2,1,0:T(8,128)}, u32[]{:S(2)}) copy-start(f32[2,2,128,128]{3,2,1,0:T(8,128)} %param.8) | copy-start | bytes 786436
  80.7 4.4 %copy-start = (f32[4096,128]{1,0:T(8,128)}, f32[4096,128]{1,0:T(8,128)S(1)}, u32[]{:S(2)}) copy-start(f32[4096,128]{1,0:T(8,128)S(1)} %fusion.47) | copy-start | bytes 6291460
  80.7 4.4 %collective-permute-start = (f32[4096,128]{1,0:T(8,128)S(1)}, f32[4096,128]{1,0:T(8,128)}, u32[]{:S(2)}, u32[]{:S(2)}) collective-permute-start(f32[4096,128]{1,0:T(8,128)S(1)} %fusion.47), channel_id=1, source_target_pairs={{0,1},{1,0},{2,3},{3,2},{4,5},{5,4},{6,7},{7,6},{8,9},{9,8},{10,11... | collective-permute-start | bytes 6291464 | tf_op jit(solution)/shard_map/ppermute | solution.py:11
  153.2 40.4 %collective-permute-start.1 = (f32[4096,128]{1,0:T(8,128)}, f32[4096,128]{1,0:T(8,128)S(1)}, u32[]{:S(2)}, u32[]{:S(2)}) collective-permute-start(f32[4096,128]{1,0:T(8,128)} %fusion.49), channel_id=1, source_target_pairs={{0,2},{1,3},{2,0},{3,1},{4,6},{5,7},{6,4},{7,5},{8,10},{9,11},{10,... | collective-permute-start | bytes 6291464 | tf_op jit(solution)/shard_map/ppermute | solution.py:11
  193.6 1.4 copy-start.3
  260.2 1.3 copy-start.4
Sparse Core Ops, SparseCore 0:
  268.2 65.9 reduce-scatter.1
